TPU v7x, 32 devices: a whole 2x2x4 slice. The times are simulated.
32 devices in a mesh: state: 8 (over z, y), mem: 4 (over x, core).
Axes of the slice: x: 2, y: 2, z: 4, core: 2. Of those that a mesh axis runs over, the one named last changes fastest.
Arguments:
- background_matrix: float32 [80, 524288], P('mem', 'state'), may hold values from -6 to 6
- measured_readings: float32 [4, 192], replicated, may hold values from -8 to 8
- measurement_noise: float32 [4, 192], replicated, may hold values from 0.5 to 2
- holding_processor: int32 [4], replicated, may hold values from 0 to 31
- measured_position: int32 [4, 192], replicated, may hold values from 0 to 16383
- taper_grade: int32 [4, 192, 1024], P(None, None, ('state', 'mem')), may hold values from 0 to 4
Outputs:
- analysis: float32 [80, 524288], P(None, ('state', 'mem'))
Inputs may be any that keep to these rules, and one draw needn't show every extreme that they name: `holding_processor`: batches may share an owner; observations of a batch may share a variable.
All inputs are finite; a program needn't handle non-finite values.
Results may differ from a plain program's by a relative error of at most 0.0003.
Values sent between devices are 32-bit elements; how exact they have to be, the bound alone decides.
No kernel may reach another device: no remote copies, remote signals or barrier semaphores. Data moves between devices by JAX's collectives and lax.ppermute only.
A program may use at most 256 MiB of HBM per device.

v0:
```python
import jax
import jax.numpy as jnp
from jax import lax
from jax.sharding import PartitionSpec as P

BATCHES = 4
PRECISE = lax.Precision.HIGHEST


def broadcast(block, axis, source):
    block = jnp.where(lax.axis_index(axis) == source, block, jnp.zeros_like(block))
    return lax.psum(block, axis)


def system_inverse(prior, errors):
    spread = prior - jnp.mean(prior, axis=0)
    system = jnp.dot(spread.T, spread, precision=PRECISE) / (prior.shape[0] - 1) + jnp.diag(errors)
    factor = jnp.linalg.cholesky(system)
    identity = jnp.eye(system.shape[0], dtype=system.dtype)
    lower_inv = lax.linalg.triangular_solve(factor, identity, left_side=True, lower=True)
    return jnp.dot(lower_inv.T, lower_inv, precision=PRECISE)


def expand_levels(levels, block_width):
    scaled = levels.astype(jnp.float32) / 4.0
    widened = scaled[:, :, None] * jnp.ones((block_width,), jnp.float32)
    return widened.reshape(levels.shape[0], levels.shape[1] * block_width)


def update_columns(realization_slab, taper, spread, innovation, inverse):
    center = jnp.mean(realization_slab, axis=0, keepdims=True)
    anomaly = realization_slab - center
    cov = jnp.dot(spread.T, anomaly, precision=PRECISE) / (realization_slab.shape[0] - 1)
    weights = jnp.dot(inverse, taper * cov, precision=PRECISE)
    center = center + jnp.dot(innovation[None, :], weights, precision=PRECISE)
    anomaly = anomaly - 0.5 * jnp.dot(spread, weights, precision=PRECISE)
    return center + anomaly


def announce(prior, root, errors):
    shared = broadcast(prior, ("state", "mem"), root)
    return (shared, system_inverse(shared, errors))


def local(
    background_matrix,
    measured_readings,
    measurement_noise,
    holding_processor,
    measured_position,
    taper_grade,
):
    realization_slab = lax.all_to_all(
        background_matrix, "mem", split_axis=1, concat_axis=0, tiled=True
    )
    block_width = realization_slab.shape[1] // taper_grade.shape[2]
    shared, inverse = announce(
        jnp.take(realization_slab, measured_position[0], axis=1),
        holding_processor[0],
        measurement_noise[0],
    )
    for batch in range(BATCHES):
        center = jnp.mean(shared, axis=0)
        spread = shared - center
        innovation = measured_readings[batch] - center
        taper = expand_levels(taper_grade[batch], block_width)
        if batch + 1 < BATCHES:
            realization_slab = update_columns(realization_slab, taper, spread, innovation, inverse)
            next_prior = jnp.take(realization_slab, measured_position[batch + 1], axis=1)
            shared, inverse = announce(
                next_prior, holding_processor[batch + 1], measurement_noise[batch + 1]
            )
        else:
            realization_slab = update_columns(realization_slab, taper, spread, innovation, inverse)
    return realization_slab


def solution(mesh):
    return jax.shard_map(
        local,
        mesh=mesh,
        in_specs=(P("mem", "state"), P(), P(), P(), P(), P(None, None, ("state", "mem"))),
        out_specs=P(None, ("state", "mem")),
        check_vma=False,
    )
```

profile of v0, /device:TPU:0, one launch (start us, length us, event | category | flops | bytes accessed | tf_op | source)
XLA Modules:
  0.0 761.5 jit_solution(15877180458151621214)
XLA Ops:
  25.7 20.4 %copy.45 = f32[24,8,32,512]{3,1,2,0:T(8,128)} copy(f32[24,8,32,512]{3,2,1,0:T(8,128)} %bitcast.185) | data formatting | bytes 25165824
  53.5 20.6 %copy.46 = f32[24,8,32,512]{3,1,2,0:T(8,128)} copy(f32[24,8,32,512]{3,2,1,0:T(8,128)} %bitcast.186) | data formatting | bytes 25165824
  79.9 20.4 %copy.47 = f32[24,8,32,512]{3,1,2,0:T(8,128)} copy(f32[24,8,32,512]{3,2,1,0:T(8,128)} %bitcast.187) | data formatting | bytes 25165824
  106.3 20.6 %copy.48 = f32[24,8,32,512]{3,1,2,0:T(8,128)} copy(f32[24,8,32,512]{3,2,1,0:T(8,128)} %bitcast.188) | data formatting | bytes 25165824
  143.9 43.6 %psum.28 = f32[80,192]{0,1:T(8,128)S(1)} all-reduce(f32[80,192]{0,1:T(8,128)S(1)} %bitcast_select_fusion.3), channel_id=1, replica_groups=mesh['state'=8,'mem'=4] {'state','mem'}, use_global_device_ids=true, to_apply=%region_1.3 | all-reduce | flops 15360 | bytes 122880 | tf_op jit(solution)/shard_map/psum | solution.py:12
  188.2 11.7 %cholesky.228 = f32[128,128]{1,0:T(8,128)S(1)} custom-call(f32[128,128]{1,0:T(8,128)S(1)} %cholesky.376), custom_call_target="Cholesky" | custom-call | tf_op jit(solution)/shard_map/jit(cholesky)/cholesky | solution.py:18
  199.9 9.8 %custom-call.17 = f32[1,128,128]{1,2,0:T(8,128)S(1)} custom-call(f32[1,128,128]{2,1,0:T(8,128)S(1)} %get-tuple-element.57), custom_call_target="InvertDiagBlocksLowerTriangular" | custom-call | tf_op jit(solution)/shard_map/jit(cholesky)/cholesky | solution.py:18
  218.8 19.7 %custom-call.18 = f32[2,128,128]{1,2,0:T(8,128)S(1)} custom-call(f32[2,128,128]{2,1,0:T(8,128)S(1)} %pad_maximum_fusion), custom_call_target="InvertDiagBlocksLowerTriangular" | custom-call | tf_op jit(solution)/shard_map/triangular_solve/custom-call.0 | solution.py:20
  242.8 18.8 %fusion.3 = f32[192,16384]{1,0:T(8,128)} fusion(f32[192,16384]{1,0:T(8,128)} %bitcast.192, f32[80,16384]{1,0:T(8,128)} %all_to_all.17, f32[16384]{0:T(1024)S(1)} %broadcast_multiply_fusion.3, f32[80,192]{0,1:T(8,128)S(1)} %psum.28, f32[192]{0:T(256)S(1)} %broadcast_multiply_fusion.7), kind=kOutput, calls=%fused_computation.11 | convolution fusion | flops 3027516416 | bytes 30536448 | tf_op jit(solution)/shard_map/dot_general | solution.py:33
  261.6 15.5 %fusion.131 = f32[192,16384]{1,0:T(8,128)S(1)} fusion(f32[192,192]{1,0:T(8,128)S(1)} %fusion.24, f32[192,16384]{1,0:T(8,128)} %fusion.3), kind=kOutput, calls=%fused_computation.247 | convolution fusion | flops 7247757312 | bytes 25313280 | tf_op jit(solution)/shard_map/dot_general | solution.py:34
  283.2 10.4 %fusion.128 = (f32[16384]{0:T(1024)S(1)}, f32[80,16384]{1,0:T(8,128)}) fusion(f32[192,16384]{1,0:T(8,128)S(1)} %fusion.131, f32[80,192]{0,1:T(8,128)S(1)} %psum.28, f32[192]{0:T(256)S(1)} %broadcast_multiply_fusion.7, f32[80,16384]{1,0:T(8,128)S(1)} %bitcast.184, f32[16384]{0:T(1024)S(1)} %broadcast_multiply_fusion.3, f32[16384]{0:T(1024)S(1)} %fusion.121), kind=kOutput, calls=%fused_computation.244 | convolution fusion | flops 3026451456 | bytes 23327488 | tf_op jit(solution)/shard_map/dot_general | solution.py:36
  305.7 41.0 %psum.29 = f32[80,192]{0,1:T(8,128)S(1)} all-reduce(f32[80,192]{0,1:T(8,128)S(1)} %bitcast_select_fusion.2), channel_id=1, replica_groups=mesh['state'=8,'mem'=4] {'state','mem'}, use_global_device_ids=true, to_apply=%region_8.12 | all-reduce | flops 15360 | bytes 122880 | tf_op jit(solution)/shard_map/psum | solution.py:12
  347.4 11.7 %cholesky.266 = f32[128,128]{1,0:T(8,128)S(1)} custom-call(f32[128,128]{1,0:T(8,128)S(1)} %cholesky.379), custom_call_target="Cholesky" | custom-call | tf_op jit(solution)/shard_map/jit(cholesky)/cholesky | solution.py:18
  359.2 9.8 %custom-call.19 = f32[1,128,128]{1,2,0:T(8,128)S(1)} custom-call(f32[1,128,128]{2,1,0:T(8,128)S(1)} %get-tuple-element.55), custom_call_target="InvertDiagBlocksLowerTriangular" | custom-call | tf_op jit(solution)/shard_map/jit(cholesky)/cholesky | solution.py:18
  377.9 19.7 %custom-call.20 = f32[2,128,128]{1,2,0:T(8,128)S(1)} custom-call(f32[2,128,128]{2,1,0:T(8,128)S(1)} %pad_maximum_fusion.1), custom_call_target="InvertDiagBlocksLowerTriangular" | custom-call | tf_op jit(solution)/shard_map/triangular_solve/custom-call.0 | solution.py:20
  398.7 18.8 %fusion.2 = f32[192,16384]{1,0:T(8,128)} fusion(f32[192,16384]{1,0:T(8,128)} %bitcast.191, f32[80,16384]{1,0:T(8,128)} %get-tuple-element.83, f32[16384]{0:T(1024)S(1)} %broadcast_multiply_fusion.2, f32[80,192]{0,1:T(8,128)S(1)} %psum.29, f32[192]{0:T(256)S(1)} %broadcast_multiply_fusion.6), kind=kOutput, calls=%fused_computation.9 | convolution fusion | flops 3027516416 | bytes 30536448 | tf_op jit(solution)/shard_map/dot_general | solution.py:33
  417.5 15.5 %fusion.132 = f32[192,16384]{1,0:T(8,128)S(1)} fusion(f32[192,192]{1,0:T(8,128)S(1)} %fusion.28, f32[192,16384]{1,0:T(8,128)} %fusion.2), kind=kOutput, calls=%fused_computation.248 | convolution fusion | flops 7247757312 | bytes 25313280 | tf_op jit(solution)/shard_map/dot_general | solution.py:34
  439.0 10.4 %fusion.129 = (f32[16384]{0:T(1024)S(1)}, f32[80,16384]{1,0:T(8,128)}) fusion(f32[192,16384]{1,0:T(8,128)S(1)} %fusion.132, f32[80,192]{0,1:T(8,128)S(1)} %psum.29, f32[192]{0:T(256)S(1)} %broadcast_multiply_fusion.6, f32[80,16384]{1,0:T(8,128)S(1)} %bitcast.180, f32[16384]{0:T(1024)S(1)} %broadcast_multiply_fusion.2, f32[16384]{0:T(1024)S(1)} %fusion.122), kind=kOutput, calls=%fused_computation.245 | convolution fusion | flops 3026451456 | bytes 23327488 | tf_op jit(solution)/shard_map/dot_general | solution.py:36
  461.6 41.0 %psum.30 = f32[80,192]{0,1:T(8,128)S(1)} all-reduce(f32[80,192]{0,1:T(8,128)S(1)} %bitcast_select_fusion.1), channel_id=1, replica_groups=mesh['state'=8,'mem'=4] {'state','mem'}, use_global_device_ids=true, to_apply=%region_11.15 | all-reduce | flops 15360 | bytes 122880 | tf_op jit(solution)/shard_map/psum | solution.py:12
  503.3 11.7 %cholesky.304 = f32[128,128]{1,0:T(8,128)S(1)} custom-call(f32[128,128]{1,0:T(8,128)S(1)} %cholesky.382), custom_call_target="Cholesky" | custom-call | tf_op jit(solution)/shard_map/jit(cholesky)/cholesky | solution.py:18
  515.0 9.8 %custom-call.21 = f32[1,128,128]{1,2,0:T(8,128)S(1)} custom-call(f32[1,128,128]{2,1,0:T(8,128)S(1)} %get-tuple-element.53), custom_call_target="InvertDiagBlocksLowerTriangular" | custom-call | tf_op jit(solution)/shard_map/jit(cholesky)/cholesky | solution.py:18
  533.7 19.7 %custom-call.22 = f32[2,128,128]{1,2,0:T(8,128)S(1)} custom-call(f32[2,128,128]{2,1,0:T(8,128)S(1)} %pad_maximum_fusion.2), custom_call_target="InvertDiagBlocksLowerTriangular" | custom-call | tf_op jit(solution)/shard_map/triangular_solve/custom-call.0 | solution.py:20
  554.5 18.9 %fusion.1 = f32[192,16384]{1,0:T(8,128)} fusion(f32[192,16384]{1,0:T(8,128)} %bitcast.190, f32[80,16384]{1,0:T(8,128)} %get-tuple-element.87, f32[16384]{0:T(1024)S(1)} %broadcast_multiply_fusion.1, f32[80,192]{0,1:T(8,128)S(1)} %psum.30, f32[192]{0:T(256)S(1)} %broadcast_multiply_fusion.5), kind=kOutput, calls=%fused_computation.7 | convolution fusion | flops 3027516416 | bytes 30536448 | tf_op jit(solution)/shard_map/dot_general | solution.py:33
  573.5 15.5 %fusion.133 = f32[192,16384]{1,0:T(8,128)S(1)} fusion(f32[192,192]{1,0:T(8,128)S(1)} %fusion.32, f32[192,16384]{1,0:T(8,128)} %fusion.1), kind=kOutput, calls=%fused_computation.249 | convolution fusion | flops 7247757312 | bytes 25313280 | tf_op jit(solution)/shard_map/dot_general | solution.py:34
  595.0 10.4 %fusion.130 = (f32[16384]{0:T(1024)S(1)}, f32[80,16384]{1,0:T(8,128)}) fusion(f32[192,16384]{1,0:T(8,128)S(1)} %fusion.133, f32[80,192]{0,1:T(8,128)S(1)} %psum.30, f32[192]{0:T(256)S(1)} %broadcast_multiply_fusion.5, f32[80,16384]{1,0:T(8,128)S(1)} %bitcast.182, f32[16384]{0:T(1024)S(1)} %broadcast_multiply_fusion.1, f32[16384]{0:T(1024)S(1)} %fusion.123), kind=kOutput, calls=%fused_computation.246 | convolution fusion | flops 3026451456 | bytes 23327488 | tf_op jit(solution)/shard_map/dot_general | solution.py:36
  617.5 40.9 %psum.31 = f32[80,192]{0,1:T(8,128)S(1)} all-reduce(f32[80,192]{0,1:T(8,128)S(1)} %bitcast_select_fusion), channel_id=1, replica_groups=mesh['state'=8,'mem'=4] {'state','mem'}, use_global_device_ids=true, to_apply=%region_14.18 | all-reduce | flops 15360 | bytes 122880 | tf_op jit(solution)/shard_map/psum | solution.py:12
  659.2 11.7 %cholesky.342 = f32[128,128]{1,0:T(8,128)S(1)} custom-call(f32[128,128]{1,0:T(8,128)S(1)} %cholesky.385), custom_call_target="Cholesky" | custom-call | tf_op jit(solution)/shard_map/jit(cholesky)/cholesky | solution.py:18
  671.0 9.8 %custom-call.23 = f32[1,128,128]{1,2,0:T(8,128)S(1)} custom-call(f32[1,128,128]{2,1,0:T(8,128)S(1)} %get-tuple-element.51), custom_call_target="InvertDiagBlocksLowerTriangular" | custom-call | tf_op jit(solution)/shard_map/jit(cholesky)/cholesky | solution.py:18
  689.9 19.7 %custom-call.24 = f32[2,128,128]{1,2,0:T(8,128)S(1)} custom-call(f32[2,128,128]{2,1,0:T(8,128)S(1)} %pad_maximum_fusion.3), custom_call_target="InvertDiagBlocksLowerTriangular" | custom-call | tf_op jit(solution)/shard_map/triangular_solve/custom-call.0 | solution.py:20
  710.6 18.8 %fusion = f32[192,16384]{1,0:T(8,128)} fusion(f32[192,16384]{1,0:T(8,128)} %bitcast.189, f32[80,16384]{1,0:T(8,128)} %get-tuple-element.91, f32[16384]{0:T(1024)S(1)} %broadcast_multiply_fusion, f32[80,192]{0,1:T(8,128)S(1)} %psum.31, f32[192]{0:T(256)S(1)} %broadcast_multiply_fusion.4), kind=kOutput, calls=%fused_computation.5 | convolution fusion | flops 3027516416 | bytes 30536448 | tf_op jit(solution)/shard_map/dot_general | solution.py:33
  729.5 15.4 %fusion.134 = f32[192,16384]{1,0:T(8,128)S(1)} fusion(f32[192,192]{1,0:T(8,128)S(1)} %fusion.36, f32[192,16384]{1,0:T(8,128)} %fusion), kind=kOutput, calls=%fused_computation.250 | convolution fusion | flops 7247757312 | bytes 25313280 | tf_op jit(solution)/shard_map/dot_general | solution.py:34
  750.9 10.2 %fusion.5 = f32[80,16384]{1,0:T(8,128)} fusion(f32[192,16384]{1,0:T(8,128)S(1)} %fusion.134, f32[80,16384]{1,0:T(8,128)S(1)} %bitcast.178, f32[16384]{0:T(1024)S(1)} %fusion.124, f32[16384]{0:T(1024)S(1)} %broadcast_multiply_fusion, f32[80,192]{0,1:T(8,128)S(1)} %psum.31, f32[192]{0:T(256)S(1)} %broadcast_multiply_fusion.4), kind=kOutput, calls=%fused_computation.14 | convolution fusion | flops 3025157120 | bytes 23261952 | tf_op jit(solution)/shard_map/dot_general | solution.py:36
  (177 shorter events, 160.6 us)
Async XLA Ops:
  7.1 13.6 %copy-start = (s32[4,192,32]{1,2,0:T(8,128)S(1)}, s32[4,192,32]{1,2,0:T(8,128)}, u32[]{:S(2)}) copy-start(s32[4,192,32]{1,2,0:T(8,128)} %param.16) | copy-start | bytes 294916
  15.2 111.9 %all-to-all-start = ((f32[20,4,16384]{2,0,1:T(8,128)}), f32[20,4,16384]{2,0,1:T(8,128)}, u32[]{:S(2)}, u32[]{:S(2)}) async-start(f32[20,4,16384]{2,0,1:T(8,128)} %copy.24), calls=%async_computation | async-start | bytes 12582912 | tf_op jit(solution)/shard_map/all_to_all | solution.py:53
  25.7 20.4 %copy-start.2 = (s32[4]{0:T(128)S(1)}, s32[4]{0:T(128)}, u32[]{:S(2)}) copy-start(s32[4]{0:T(128)} %param.14) | copy-start | bytes 52
  106.3 20.6 %copy-start.3 = (s32[4,192]{1,0:T(4,128)S(1)}, s32[4,192]{1,0:T(4,128)}, u32[]{:S(2)}) copy-start(s32[4,192]{1,0:T(4,128)} %param.15) | copy-start | bytes 9220
  106.3 20.8 %copy-start.4 = (f32[4,192]{1,0:T(4,128)S(1)}, f32[4,192]{1,0:T(4,128)}, u32[]{:S(2)}) copy-start(f32[4,192]{1,0:T(4,128)} %param.13) | copy-start | bytes 9220
  261.6 15.5 %copy-start.1 = (f32[4,192]{1,0:T(4,128)S(1)}, f32[4,192]{1,0:T(4,128)}, u32[]{:S(2)}) copy-start(f32[4,192]{1,0:T(4,128)} %param.12) | copy-start | bytes 9220
  277.2 6.0 slice-start.6
  277.2 6.0 slice-start.7
  433.0 6.0 slice-start.2
  433.0 6.0 slice-start.3
  589.0 6.0 slice-start.4
  589.0 6.0 slice-start.5
  744.8 6.0 slice-start
  744.8 6.0 slice-start.1
where the time goes:
time: 767 us; the launch traced here: 761 us
  matrix products  210 us (27%)
  other arithmetic  198 us (26%)
  local copies, waits for them, and re-layouts  172 us (22%)
  blocking collectives  166 us (22%)
  between operations  9.04 us (1%)
    psum x4, blocking collectives, broadcast(): return lax.psum(block, axis)  166 us
    another operation x28, other arithmetic, system_inverse(): factor = jnp.linalg.cholesky(system)  115 us
    unnamed x30, local copies, waits for them, and re-layouts  82.1 us
    another operation x18, other arithmetic, system_inverse(): lax.linalg.triangular_solve(factor, identity, left_side=True, lower=True)  79.2 us
    dot_general x4, matrix products, update_columns(): jnp.dot(spread.T, anomaly, precision=PRECISE)  75.4 us
    dot_general x4, matrix products, update_columns(): weights = jnp.dot(inverse, taper * cov, precision=PRECISE)  61.9 us
    dot_general x4, matrix products, update_columns(): anomaly = anomaly - 0.5 * jnp.dot(spread, weights, precision=PRECISE)  41.4 us
    all_to_all x4, local copies, waits for them, and re-layouts, local(): lax.all_to_all(background_matrix, 'mem', split_axis=1, concat_axis=0, til...  27.8 us
  transfers between devices with their start and end apart: 1, of which 0 were waited for; matrix products, arithmetic and copies ran while one was open for 14% of the time, Pallas kernels for 0%

commit v1 on v0

--- a/solution.py
+++ b/solution.py
@@ -7,9 +7,15 @@
 PRECISE = lax.Precision.HIGHEST
 
 
+def summed_here(x, axis):
+    parts = lax.all_gather(x, axis, axis=0, tiled=False)
+    total = parts.sum(axis=0)
+    return total
+
+
 def broadcast(block, axis, source):
     block = jnp.where(lax.axis_index(axis) == source, block, jnp.zeros_like(block))
-    return lax.psum(block, axis)
+    return summed_here(block, axis)
 
 
 def system_inverse(prior, errors):

time: 767 us -> 818 us (1.066)
  waiting for transfers between devices: 0.01 us -> 190 us
  blocking collectives: 166 us -> 0 us
  other arithmetic: 198 us -> 215 us
  between operations: 9.04 us -> 22.3 us
    psum x4 -> x0, blocking collectives: 166 us -> none  [broadcast(): return lax.psum(block, axis)]
    all_gather x0 -> x4, waiting for transfers between devices: none -> 120 us  [summed_here(): parts = lax.all_gather(x, axis, axis=0, tiled=False)]
    all_to_all x1, waiting for transfers between devices: 0.01 us -> 69.8 us  [local(): lax.all_to_all(background_matrix, 'mem', split_axis=1, concat_axis=0, til...]
    reduce_sum x4, other arithmetic: 0.41 us -> 8.77 us  [local(): center = jnp.mean(shared, axis=0)]
  transfers between devices with their start and end apart: 1 -> 5, of which waited for: 0 -> 5; matrix products, arithmetic and copies ran while one was open for 14% -> 13% of each run, Pallas kernels for 0% -> 0%
where the time goes in v1:
time: 818 us; the launch traced here: 811 us
  other arithmetic  215 us (26%)
  matrix products  203 us (25%)
  waiting for transfers between devices  190 us (23%)
  local copies, waits for them, and re-layouts  175 us (21%)
  between operations  22.3 us (3%)
    all_gather x4, waiting for transfers between devices, summed_here(): parts = lax.all_gather(x, axis, axis=0, tiled=False)  120 us
    another operation x28, other arithmetic, system_inverse(): factor = jnp.linalg.cholesky(system)  115 us
    unnamed x30, local copies, waits for them, and re-layouts  82.6 us
    another operation x18, other arithmetic, system_inverse(): lax.linalg.triangular_solve(factor, identity, left_side=True, lower=True)  79.2 us
    dot_general x4, matrix products, update_columns(): jnp.dot(spread.T, anomaly, precision=PRECISE)  69.9 us
    all_to_all x1, waiting for transfers between devices, local(): lax.all_to_all(background_matrix, 'mem', split_axis=1, concat_axis=0, til...  69.8 us
    dot_general x4, matrix products, update_columns(): weights = jnp.dot(inverse, taper * cov, precision=PRECISE)  61.4 us
    dot_general x4, matrix products, update_columns(): anomaly = anomaly - 0.5 * jnp.dot(spread, weights, precision=PRECISE)  40 us
  transfers between devices with their start and end apart: 5, of which 5 were waited for; matrix products, arithmetic and copies ran while one was open for 13% of the time, Pallas kernels for 0%

profile of v1, /device:TPU:0, one launch (start us, length us, event | category | flops | bytes accessed | tf_op | source)
XLA Modules:
  0.0 810.7 jit_solution(7148612966748265112)
XLA Ops:
  28.7 69.8 %all-to-all-done = f32[20,4,16384]{2,0,1:T(8,128)} async-done(((f32[20,4,16384]{2,0,1:T(8,128)}), f32[20,4,16384]{2,0,1:T(8,128)}, u32[]{:S(2)}, u32[]{:S(2)}) %all-to-all-start) | async-done | bytes 5242912 | tf_op jit(solution)/shard_map/all_to_all | solution.py:59
  121.2 20.6 %copy.86 = f32[24,8,32,512]{3,1,2,0:T(8,128)} copy(f32[24,8,32,512]{3,2,1,0:T(8,128)} %bitcast.193) | data formatting | bytes 25165824
  145.8 29.3 %all-gather.9.cloned.1.call-done = f32[2560,192]{1,0:T(8,128)} async-done(((f32[80,192]{1,0:T(8,128)}), f32[2560,192]{1,0:T(8,128)}) %all-gather.9.cloned.1.call-update) | async-done | bytes 1966096 | tf_op jit(solution)/shard_map/all_gather | solution.py:11
  179.8 11.7 %cholesky.228 = f32[128,128]{1,0:T(8,128)S(1)} custom-call(f32[128,128]{1,0:T(8,128)S(1)} %cholesky.376), custom_call_target="Cholesky" | custom-call | tf_op jit(solution)/shard_map/jit(cholesky)/cholesky | solution.py:24
  191.6 9.8 %custom-call.17 = f32[1,128,128]{1,2,0:T(8,128)S(1)} custom-call(f32[1,128,128]{2,1,0:T(8,128)S(1)} %get-tuple-element.57), custom_call_target="InvertDiagBlocksLowerTriangular" | custom-call | tf_op jit(solution)/shard_map/jit(cholesky)/cholesky | solution.py:24
  210.5 19.7 %custom-call.18 = f32[2,128,128]{1,2,0:T(8,128)S(1)} custom-call(f32[2,128,128]{2,1,0:T(8,128)S(1)} %pad_maximum_fusion), custom_call_target="InvertDiagBlocksLowerTriangular" | custom-call | tf_op jit(solution)/shard_map/triangular_solve/custom-call.0 | solution.py:26
  231.2 17.6 %fusion.3 = f32[192,16384]{1,0:T(8,128)} fusion(f32[192,16384]{1,0:T(8,128)} %bitcast.189, f32[80,16384]{1,0:T(8,128)} %all_to_all.17, f32[16384]{0:T(1024)S(1)} %broadcast_multiply_fusion.3, f32[80,192]{1,0:T(8,128)S(1)} %reduce_sum.107, f32[192]{0:T(256)S(1)} %broadcast_multiply_fusion.7), kind=kOutput, calls=%fused_computation.11 | convolution fusion | flops 3027516416 | bytes 30536448 | tf_op jit(solution)/shard_map/dot_general | solution.py:39
  248.8 15.3 %fusion.131 = f32[192,16384]{1,0:T(8,128)S(1)} fusion(f32[192,192]{1,0:T(8,128)S(1)} %fusion.24, f32[192,16384]{1,0:T(8,128)} %fusion.3), kind=kOutput, calls=%fused_computation.247 | convolution fusion | flops 7247757312 | bytes 25313280 | tf_op jit(solution)/shard_map/dot_general | solution.py:40
  270.2 10.1 %fusion.128 = (f32[16384]{0:T(1024)S(1)}, f32[80,16384]{1,0:T(8,128)}) fusion(f32[192,16384]{1,0:T(8,128)S(1)} %fusion.131, f32[80,192]{1,0:T(8,128)S(1)} %reduce_sum.107, f32[192]{0:T(256)S(1)} %broadcast_multiply_fusion.7, f32[80,16384]{1,0:T(8,128)S(1)} %bitcast.182, f32[16384]{0:T(1024)S(1)} %broadcast_multiply_fusion.3, f32[16384]{0:T(1024)S(1)} %fusion.121), kind=kOutput, calls=%fused_computation.244 | convolution fusion | flops 3026451456 | bytes 23327488 | tf_op jit(solution)/shard_map/dot_general | solution.py:42
  298.3 20.6 %copy.87 = f32[24,8,32,512]{3,1,2,0:T(8,128)} copy(f32[24,8,32,512]{3,2,1,0:T(8,128)} %bitcast.194) | data formatting | bytes 25165824
  319.7 30.0 %all-gather.11.cloned.1.call-done = f32[2560,192]{1,0:T(8,128)} async-done(((f32[80,192]{1,0:T(8,128)}), f32[2560,192]{1,0:T(8,128)}) %all-gather.11.cloned.1.call-update) | async-done | bytes 1966096 | tf_op jit(solution)/shard_map/all_gather | solution.py:11
  354.7 11.7 %cholesky.266 = f32[128,128]{1,0:T(8,128)S(1)} custom-call(f32[128,128]{1,0:T(8,128)S(1)} %cholesky.379), custom_call_target="Cholesky" | custom-call | tf_op jit(solution)/shard_map/jit(cholesky)/cholesky | solution.py:24
  366.4 9.8 %custom-call.19 = f32[1,128,128]{1,2,0:T(8,128)S(1)} custom-call(f32[1,128,128]{2,1,0:T(8,128)S(1)} %get-tuple-element.55), custom_call_target="InvertDiagBlocksLowerTriangular" | custom-call | tf_op jit(solution)/shard_map/jit(cholesky)/cholesky | solution.py:24
  385.3 19.7 %custom-call.20 = f32[2,128,128]{1,2,0:T(8,128)S(1)} custom-call(f32[2,128,128]{2,1,0:T(8,128)S(1)} %pad_maximum_fusion.1), custom_call_target="InvertDiagBlocksLowerTriangular" | custom-call | tf_op jit(solution)/shard_map/triangular_solve/custom-call.0 | solution.py:26
  406.1 17.4 %fusion.2 = f32[192,16384]{1,0:T(8,128)} fusion(f32[192,16384]{1,0:T(8,128)} %bitcast.190, f32[80,16384]{1,0:T(8,128)} %get-tuple-element.83, f32[16384]{0:T(1024)S(1)} %broadcast_multiply_fusion.2, f32[80,192]{1,0:T(8,128)S(1)} %reduce_sum.129, f32[192]{0:T(256)S(1)} %broadcast_multiply_fusion.6), kind=kOutput, calls=%fused_computation.9 | convolution fusion | flops 3027516416 | bytes 30536448 | tf_op jit(solution)/shard_map/dot_general | solution.py:39
  423.5 15.3 %fusion.132 = f32[192,16384]{1,0:T(8,128)S(1)} fusion(f32[192,192]{1,0:T(8,128)S(1)} %fusion.28, f32[192,16384]{1,0:T(8,128)} %fusion.2), kind=kOutput, calls=%fused_computation.248 | convolution fusion | flops 7247757312 | bytes 25313280 | tf_op jit(solution)/shard_map/dot_general | solution.py:40
  444.8 10.1 %fusion.129 = (f32[16384]{0:T(1024)S(1)}, f32[80,16384]{1,0:T(8,128)}) fusion(f32[192,16384]{1,0:T(8,128)S(1)} %fusion.132, f32[80,192]{1,0:T(8,128)S(1)} %reduce_sum.129, f32[192]{0:T(256)S(1)} %broadcast_multiply_fusion.6, f32[80,16384]{1,0:T(8,128)S(1)} %bitcast.184, f32[16384]{0:T(1024)S(1)} %broadcast_multiply_fusion.2, f32[16384]{0:T(1024)S(1)} %fusion.122), kind=kOutput, calls=%fused_computation.245 | convolution fusion | flops 3026451456 | bytes 23327488 | tf_op jit(solution)/shard_map/dot_general | solution.py:42
  473.1 20.6 %copy.88 = f32[24,8,32,512]{3,1,2,0:T(8,128)} copy(f32[24,8,32,512]{3,2,1,0:T(8,128)} %bitcast.195) | data formatting | bytes 25165824
  494.5 29.9 %all-gather.13.cloned.1.call-done = f32[2560,192]{1,0:T(8,128)} async-done(((f32[80,192]{1,0:T(8,128)}), f32[2560,192]{1,0:T(8,128)}) %all-gather.13.cloned.1.call-update) | async-done | bytes 1966096 | tf_op jit(solution)/shard_map/all_gather | solution.py:11
  529.1 11.7 %cholesky.304 = f32[128,128]{1,0:T(8,128)S(1)} custom-call(f32[128,128]{1,0:T(8,128)S(1)} %cholesky.382), custom_call_target="Cholesky" | custom-call | tf_op jit(solution)/shard_map/jit(cholesky)/cholesky | solution.py:24
  540.9 9.8 %custom-call.21 = f32[1,128,128]{1,2,0:T(8,128)S(1)} custom-call(f32[1,128,128]{2,1,0:T(8,128)S(1)} %get-tuple-element.53), custom_call_target="InvertDiagBlocksLowerTriangular" | custom-call | tf_op jit(solution)/shard_map/jit(cholesky)/cholesky | solution.py:24
  559.8 19.7 %custom-call.22 = f32[2,128,128]{1,2,0:T(8,128)S(1)} custom-call(f32[2,128,128]{2,1,0:T(8,128)S(1)} %pad_maximum_fusion.2), custom_call_target="InvertDiagBlocksLowerTriangular" | custom-call | tf_op jit(solution)/shard_map/triangular_solve/custom-call.0 | solution.py:26
  580.5 17.4 %fusion.1 = f32[192,16384]{1,0:T(8,128)} fusion(f32[192,16384]{1,0:T(8,128)} %bitcast.191, f32[80,16384]{1,0:T(8,128)} %get-tuple-element.87, f32[16384]{0:T(1024)S(1)} %broadcast_multiply_fusion.1, f32[80,192]{1,0:T(8,128)S(1)} %reduce_sum.132, f32[192]{0:T(256)S(1)} %broadcast_multiply_fusion.5), kind=kOutput, calls=%fused_computation.7 | convolution fusion | flops 3027516416 | bytes 30536448 | tf_op jit(solution)/shard_map/dot_general | solution.py:39
  597.9 15.5 %fusion.133 = f32[192,16384]{1,0:T(8,128)S(1)} fusion(f32[192,192]{1,0:T(8,128)S(1)} %fusion.32, f32[192,16384]{1,0:T(8,128)} %fusion.1), kind=kOutput, calls=%fused_computation.249 | convolution fusion | flops 7247757312 | bytes 25313280 | tf_op jit(solution)/shard_map/dot_general | solution.py:40
  619.5 10.1 %fusion.130 = (f32[16384]{0:T(1024)S(1)}, f32[80,16384]{1,0:T(8,128)}) fusion(f32[192,16384]{1,0:T(8,128)S(1)} %fusion.133, f32[80,192]{1,0:T(8,128)S(1)} %reduce_sum.132, f32[192]{0:T(256)S(1)} %broadcast_multiply_fusion.5, f32[80,16384]{1,0:T(8,128)S(1)} %bitcast.186, f32[16384]{0:T(1024)S(1)} %broadcast_multiply_fusion.1, f32[16384]{0:T(1024)S(1)} %fusion.123), kind=kOutput, calls=%fused_computation.246 | convolution fusion | flops 3026451456 | bytes 23327488 | tf_op jit(solution)/shard_map/dot_general | solution.py:42
  647.5 20.6 %copy.89 = f32[24,8,32,512]{3,1,2,0:T(8,128)} copy(f32[24,8,32,512]{3,2,1,0:T(8,128)} %bitcast.196) | data formatting | bytes 25165824
  668.2 30.8 %all-gather.15.cloned.1.call-done = f32[2560,192]{1,0:T(8,128)} async-done(((f32[80,192]{1,0:T(8,128)}), f32[2560,192]{1,0:T(8,128)}) %all-gather.15.cloned.1.call-update) | async-done | bytes 1966096 | tf_op jit(solution)/shard_map/all_gather | solution.py:11
  703.8 11.7 %cholesky.342 = f32[128,128]{1,0:T(8,128)S(1)} custom-call(f32[128,128]{1,0:T(8,128)S(1)} %cholesky.385), custom_call_target="Cholesky" | custom-call | tf_op jit(solution)/shard_map/jit(cholesky)/cholesky | solution.py:24
  734.4 19.7 %custom-call.24 = f32[2,128,128]{1,2,0:T(8,128)S(1)} custom-call(f32[2,128,128]{2,1,0:T(8,128)S(1)} %pad_maximum_fusion.3), custom_call_target="InvertDiagBlocksLowerTriangular" | custom-call | tf_op jit(solution)/shard_map/triangular_solve/custom-call.0 | solution.py:26
  755.2 17.6 %fusion = f32[192,16384]{1,0:T(8,128)} fusion(f32[192,16384]{1,0:T(8,128)} %bitcast.192, f32[80,16384]{1,0:T(8,128)} %get-tuple-element.91, f32[16384]{0:T(1024)S(1)} %broadcast_multiply_fusion, f32[80,192]{1,0:T(8,128)S(1)} %reduce_sum.135, f32[192]{0:T(256)S(1)} %broadcast_multiply_fusion.4), kind=kOutput, calls=%fused_computation.5 | convolution fusion | flops 3027516416 | bytes 30536448 | tf_op jit(solution)/shard_map/dot_general | solution.py:39
  772.8 15.3 %fusion.134 = f32[192,16384]{1,0:T(8,128)S(1)} fusion(f32[192,192]{1,0:T(8,128)S(1)} %fusion.36, f32[192,16384]{1,0:T(8,128)} %fusion), kind=kOutput, calls=%fused_computation.250 | convolution fusion | flops 7247757312 | bytes 25313280 | tf_op jit(solution)/shard_map/dot_general | solution.py:40
  794.1 9.8 %fusion.5 = f32[80,16384]{1,0:T(8,128)} fusion(f32[192,16384]{1,0:T(8,128)S(1)} %fusion.134, f32[80,16384]{1,0:T(8,128)S(1)} %bitcast.188, f32[16384]{0:T(1024)S(1)} %fusion.124, f32[16384]{0:T(1024)S(1)} %broadcast_multiply_fusion, f32[80,192]{1,0:T(8,128)S(1)} %reduce_sum.135, f32[192]{0:T(256)S(1)} %broadcast_multiply_fusion.4), kind=kOutput, calls=%fused_computation.14 | convolution fusion | flops 3025157120 | bytes 23261952 | tf_op jit(solution)/shard_map/dot_general | solution.py:42
  (192 shorter events, 189.8 us)
Async XLA Ops:
  21.8 5.5 copy-start.2
  21.8 6.9 copy-start.3
  21.8 76.7 %all-to-all-start = ((f32[20,4,16384]{2,0,1:T(8,128)}), f32[20,4,16384]{2,0,1:T(8,128)}, u32[]{:S(2)}, u32[]{:S(2)}) async-start(f32[20,4,16384]{2,0,1:T(8,128)} %copy.45), calls=%async_computation | async-start | bytes 12582912 | tf_op jit(solution)/shard_map/all_to_all | solution.py:59
  27.3 147.8 %all-gather.9.cloned.1.call-start = ((), (), s32[]{:S(2)}) async-start(), calls=%async_computation.1 | async-start | bytes 2703360 | tf_op jit(solution)/shard_map/all_gather | solution.py:11
  103.1 12.9 %copy-start = (s32[4,192,32]{1,2,0:T(8,128)S(1)}, s32[4,192,32]{1,2,0:T(8,128)}, u32[]{:S(2)}) copy-start(s32[4,192,32]{1,2,0:T(8,128)} %param.16) | copy-start | bytes 294916
  116.0 233.7 %all-gather.11.cloned.1.call-start = ((), (), s32[]{:S(2)}) async-start(), calls=%async_computation.2 | async-start | bytes 2703360 | tf_op jit(solution)/shard_map/all_gather | solution.py:11
  121.2 21.3 %copy-start.4 = (f32[4,192]{1,0:T(4,128)S(1)}, f32[4,192]{1,0:T(4,128)}, u32[]{:S(2)}) copy-start(f32[4,192]{1,0:T(4,128)} %param.13) | copy-start | bytes 9220
  248.8 15.3 %copy-start.1 = (f32[4,192]{1,0:T(4,128)S(1)}, f32[4,192]{1,0:T(4,128)}, u32[]{:S(2)}) copy-start(f32[4,192]{1,0:T(4,128)} %param.12) | copy-start | bytes 9220
  264.1 6.0 slice-start
  264.1 6.0 slice-start.1
  293.1 231.3 %all-gather.13.cloned.1.call-start = ((), (), s32[]{:S(2)}) async-start(), calls=%async_computation.3 | async-start | bytes 2703360 | tf_op jit(solution)/shard_map/all_gather | solution.py:11
  438.8 6.0 slice-start.2
  438.8 6.0 slice-start.3
  467.8 231.3 %all-gather.15.cloned.1.call-start = ((), (), s32[]{:S(2)}) async-start(), calls=%async_computation.4 | async-start | bytes 2703360 | tf_op jit(solution)/shard_map/all_gather | solution.py:11
  613.4 6.0 slice-start.4
  613.5 6.0 slice-start.5
  788.1 6.0 slice-start.6
  788.1 6.0 slice-start.7
Sparse Core Ops, SparseCore 0:
  116.2 58.8 all-gather.8
  293.2 56.4 all-gather.10
  467.9 56.4 all-gather.12
  642.5 56.4 all-gather.14
